TPU v7x, 256 devices: a whole 4x4x8 slice. The times are simulated.
256 devices in a mesh: cuts: 16 (over z, core), rank: 16 (over x, y).
Axes of the slice: x: 4, y: 4, z: 8, core: 2. Of those that a mesh axis runs over, the one named last changes fastest.
Arguments:
- core_one: float32 [512, 320, 512], P('rank', 'cuts'), may hold values from -6 to 6
- core_two: float32 [512, 320, 512], P('rank', 'cuts'), may hold values from -0.25 to 0.25
- right_sketch: float32 [512, 128], replicated, may hold values from -0.25 to 0.25
- sketch_core: float32 [128, 320, 128], P(None, 'cuts'), may hold values from -0.03125 to 0.03125
Outputs:
- left_core: float32 [512, 320, 128], P('rank', 'cuts')
- middle_core: float32 [128, 320, 128], P('rank', 'cuts')
- carry: float32 [128, 512], replicated
All inputs are finite; a program needn't handle non-finite values.
Results may differ from a plain program's by a relative error of at most 0.00015.
Values sent between devices are 32-bit elements; how exact they have to be, the bound alone decides.
A program may use at most 64 MiB of HBM per device.

v0:
```python
import jax
import jax.numpy as jnp
from jax import lax
from jax.sharding import PartitionSpec as P

R = 512
NM = 320
L = 128


def orthonormalize(all_rows, own_rows, carry_of):
    highest = lax.Precision.HIGHEST
    local_gram = jnp.dot(
        own_rows.T, own_rows, precision=highest, preferred_element_type=jnp.float32
    )
    gram = lax.psum(local_gram, ("cuts", "rank"))
    factor = jnp.linalg.cholesky(gram)
    ortho = lax.linalg.triangular_solve(
        factor, all_rows, left_side=False, lower=True, transpose_a=True
    )
    carried = lax.psum(carry_of(ortho), ("cuts", "rank"))
    return (ortho, carried)


def on_device(core_one, core_two, right_sketch, sketch_core):
    highest = lax.Precision.HIGHEST
    local_rows, slices, width = core_one.shape
    sketch_width = right_sketch.shape[1]
    band = sketch_width // lax.axis_size("rank")
    sketched = jnp.einsum("anj,jc->anc", core_two, right_sketch, precision=highest)
    part_bridge = jnp.einsum("anc,bnc->ab", sketched, sketch_core, precision=highest)
    bridge_rows = lax.psum(part_bridge, "cuts")
    flat_one = core_one.reshape(local_rows * slices, width)
    first_rows = jnp.dot(
        flat_one,
        lax.all_gather(bridge_rows, "rank", axis=0, tiled=True),
        precision=highest,
        preferred_element_type=jnp.float32,
    )

    def first_carry_of(matrix):
        return jnp.dot(matrix.T, flat_one, precision=highest, preferred_element_type=jnp.float32)

    first_q, first_carry = orthonormalize(first_rows, first_rows, first_carry_of)
    left_core = (jnp.sqrt(jnp.float32(R * NM)) * first_q).reshape(local_rows, slices, sketch_width)
    offset = lax.axis_index("rank") * local_rows
    local_carry = lax.dynamic_slice_in_dim(first_carry, offset, local_rows, 1)
    projected = lax.psum_scatter(
        jnp.einsum("ba,ank->bnk", local_carry, core_two, precision=highest),
        "rank",
        scatter_dimension=0,
        tiled=True,
    )
    flat_two = projected.reshape(band * slices, width)
    second_rows = jnp.dot(
        flat_two, right_sketch, precision=highest, preferred_element_type=jnp.float32
    )

    def second_carry_of(matrix):
        return jnp.dot(matrix.T, flat_two, precision=highest, preferred_element_type=jnp.float32)

    second_flat, carry = orthonormalize(second_rows, second_rows, second_carry_of)
    second_q = second_flat.reshape(band, slices, sketch_width)
    middle_core = jnp.sqrt(jnp.float32(L * NM)) * second_q
    return (left_core, middle_core, carry)


def solution(mesh):
    placed = (P("rank", "cuts", None), P("rank", "cuts", None), P(), P(None, "cuts", None))
    return jax.shard_map(
        on_device,
        mesh=mesh,
        in_specs=placed,
        out_specs=(P("rank", "cuts", None), P("rank", "cuts", None), P()),
        check_vma=False,
    )
```

profile of v0, /device:TPU:2, one launch (start us, length us, event | category | flops | bytes accessed | tf_op | source)
XLA Modules:
  0.0 1233.6 jit_solution(7768651899658973247)
XLA Ops:
  7.2 0.0 copy-start
  7.2 0.0 copy-start.1
  7.2 0.0 all-reduce.5.cloned.1.call-start
  7.2 1.3 copy-done
  8.5 2.1 fusion
  10.6 0.0 copy-done.1
  10.6 1.4 convolution_bitcast_fusion
  12.0 50.9 %psum.35 = f32[32,128]{1,0:T(8,128)S(1)} all-reduce(f32[32,128]{1,0:T(8,128)S(1)} %convolution_bitcast_fusion), channel_id=1, replica_groups=mesh['cuts'=16,'rank'=16] {'cuts'}, use_global_device_ids=true, to_apply=%region_0.0 | all-reduce | flops 4096 | bytes 32768 | tf_op jit(solution)/shard_map/psum | solution.py:32
  62.9 23.8 %all_gather.3 = f32[512,128]{1,0:T(8,128)S(1)} all-gather(f32[32,128]{1,0:T(8,128)S(1)} %psum.35), channel_id=1, replica_groups=mesh['cuts'=16,'rank'=16] {'rank'}, dimensions={0}, use_global_device_ids=true | all-gather | bytes 278528 | tf_op jit(solution)/shard_map/all_gather | solution.py:36
  86.7 3.2 copy.13
  89.9 1.5 reshape.29
  91.4 1.6 fusion.14
  92.9 1.1 fusion.15
  94.0 0.0 all-reduce.5.cloned.1.call-update
  94.1 0.2 all-reduce.7.cloned.1.call-start
  94.3 236.5 %all-reduce.5.cloned.1.call-done = f32[128,128]{0,1:T(8,128)} async-done(((f32[128,128]{0,1:T(8,128)}), f32[128,128]{0,1:T(8,128)}) %all-reduce.5.cloned.1.call-update) | async-done | bytes 65552 | tf_op jit(solution)/shard_map/psum | solution.py:16
  330.8 0.9 copy.15
  331.8 0.9 fusion.9
  332.6 11.7 cholesky.44
  344.4 0.6 compare_reduce_fusion.1
  345.0 0.7 fusion.2
  345.7 9.8 custom-call.8
  355.5 0.7 broadcast_multiply_fusion
  356.2 3.0 fusion.16
  359.2 0.0 all-reduce.7.cloned.1.call-update
  359.2 0.0 reduce-scatter.2.cloned.1.call-start
  359.2 251.8 %all-reduce.7.cloned.1.call-done = f32[128,512]{0,1:T(8,128)} async-done(((f32[128,512]{0,1:T(8,128)}), f32[128,512]{0,1:T(8,128)}) %all-reduce.7.cloned.1.call-update) | async-done | bytes 262160 | tf_op jit(solution)/shard_map/psum | solution.py:21
  611.0 6.8 fusion.10
  617.8 0.0 reduce-scatter.2.cloned.1.call-update
  617.8 0.0 copy-start.2
  617.8 0.3 all-reduce.9.cloned.1.call-start
  618.1 83.2 %reduce-scatter.2.cloned.1.call-done = f32[8,20,512]{2,0,1:T(8,128)} async-done(((f32[128,20,512]{2,0,1:T(8,128)}), f32[8,20,512]{2,0,1:T(8,128)}) %reduce-scatter.2.cloned.1.call-update) | async-done | bytes 327696 | tf_op jit(solution)/shard_map/reduce_scatter | solution.py:48
  701.3 1.2 copy.16
  702.5 0.0 copy-done.2
  702.5 0.4 fusion.17
  703.0 1.1 fusion.18
  704.0 0.0 all-reduce.9.cloned.1.call-update
  704.1 0.0 all-reduce.11.cloned.1.call-start
  704.1 243.4 %all-reduce.9.cloned.1.call-done = f32[128,128]{0,1:T(8,128)} async-done(((f32[128,128]{0,1:T(8,128)}), f32[128,128]{0,1:T(8,128)}) %all-reduce.9.cloned.1.call-update) | async-done | bytes 65552 | tf_op jit(solution)/shard_map/psum | solution.py:16
  947.6 0.9 copy.18
  948.5 0.9 fusion.6
  949.3 11.7 cholesky.55
  961.1 0.6 compare_reduce_fusion
  961.7 0.7 fusion.3
  962.4 9.8 custom-call.9
  972.2 0.2 broadcast_multiply_fusion.1
  972.4 1.1 fusion.19
  973.6 0.0 all-reduce.11.cloned.1.call-update
  973.6 0.8 copy.19
  974.4 0.7 copy.20
  975.1 250.3 %all-reduce.11.cloned.1.call-done = f32[128,512]{1,0:T(8,128)} async-done(((f32[128,512]{1,0:T(8,128)}), f32[128,512]{1,0:T(8,128)}) %all-reduce.11.cloned.1.call-update) | async-done | bytes 262160 | tf_op jit(solution)/shard_map/psum | solution.py:21
  1225.4 1.7 copy.29
  (5 shorter events, 0.1 us)
Async XLA Ops:
  7.2 1.3 copy-start
  7.2 3.4 copy-start.1
  7.2 323.6 %all-reduce.5.cloned.1.call-start = ((), (), s32[]{:S(2)}) async-start(), calls=%async_computation.1 | async-start | bytes 131072 | tf_op jit(solution)/shard_map/psum | solution.py:16
  94.1 516.9 %all-reduce.7.cloned.1.call-start = ((), (), s32[]{:S(2)}) async-start(), calls=%async_computation.2 | async-start | bytes 524288 | tf_op jit(solution)/shard_map/psum | solution.py:21
  359.2 342.1 %reduce-scatter.2.cloned.1.call-start = ((), (), s32[]{:S(2)}) async-start(), calls=%async_computation.3 | async-start | bytes 5570560 | tf_op jit(solution)/shard_map/reduce_scatter | solution.py:48
  617.8 84.7 %copy-start.2 = (f32[512,128]{1,0:T(8,128)S(1)}, f32[512,128]{1,0:T(8,128)}, u32[]{:S(2)}) copy-start(f32[512,128]{1,0:T(8,128)} %param.7) | copy-start | bytes 786436
  617.8 329.7 %all-reduce.9.cloned.1.call-start = ((), (), s32[]{:S(2)}) async-start(), calls=%async_computation.4 | async-start | bytes 131072 | tf_op jit(solution)/shard_map/psum | solution.py:16
  704.1 521.3 %all-reduce.11.cloned.1.call-start = ((), (), s32[]{:S(2)}) async-start(), calls=%async_computation.5 | async-start | bytes 524288 | tf_op jit(solution)/shard_map/psum | solution.py:21
Sparse Core Ops, SparseCore 0:
  94.2 236.5 all-reduce.4
  359.3 251.6 all-reduce.6
  617.9 83.3 reduce-scatter.1
  707.3 240.2 all-reduce.8
  973.7 251.5 all-reduce.10
where the time goes:
time: 1230 us
  waiting for transfers between devices  1070 us (87%)
  blocking collectives  74.6 us (6%)
  other arithmetic  47.4 us (4%)
  matrix products  19.5 us (2%)
  between operations  13.9 us (1%)
    psum x2, waiting for transfers between devices, orthonormalize(): carried = lax.psum(carry_of(ortho), ('cuts', 'rank'))  502 us
    psum x2, waiting for transfers between devices, orthonormalize(): gram = lax.psum(local_gram, ('cuts', 'rank'))  480 us
    reduce_scatter x1, waiting for transfers between devices, on_device(): lax.psum_scatter(jnp.einsum('ba,ank->bnk', local_carry, core_two, precisi...  83.2 us
    psum x1, blocking collectives, on_device(): bridge_rows = lax.psum(part_bridge, 'cuts')  50.9 us
    another operation x6, other arithmetic, orthonormalize(): factor = jnp.linalg.cholesky(gram)  24.8 us
  transfers between devices with their start and end apart: 5, of which 5 were waited for; matrix products, arithmetic and copies ran while one was open for 0% of the time, Pallas kernels for 0%

commit v1 on v0

--- a/solution.py
+++ b/solution.py
@@ -18,7 +18,7 @@
     ortho = lax.linalg.triangular_solve(
         factor, all_rows, left_side=False, lower=True, transpose_a=True
     )
-    carried = lax.psum(carry_of(ortho), ("cuts", "rank"))
+    carried = lax.psum(lax.psum(carry_of(ortho), "rank"), "cuts")
     return (ortho, carried)
 
 

time: 1230 us -> 1140 us (0.927)
  waiting for transfers between devices: 1070 us -> 972 us
    psum x2 -> x4, waiting for transfers between devices: 502 us -> 407 us  [orthonormalize(): carried = lax.psum(lax.psum(carry_of(ortho), 'rank'), 'cuts')]
  transfers between devices with their start and end apart: 5 -> 7, of which waited for: 5 -> 7; matrix products, arithmetic and copies ran while one was open for 0% -> 0% of each run, Pallas kernels for 0% -> 0%
where the time goes in v1:
time: 1140 us
  waiting for transfers between devices  972 us (85%)
  blocking collectives  74.6 us (7%)
  other arithmetic  47.4 us (4%)
  matrix products  19.5 us (2%)
  between operations  14.3 us (1%)
  local copies, waits for them, and re-layouts  12.2 us (1%)
    psum x2, waiting for transfers between devices, orthonormalize(): gram = lax.psum(local_gram, ('cuts', 'rank'))  480 us
    psum x4, waiting for transfers between devices, orthonormalize(): carried = lax.psum(lax.psum(carry_of(ortho), 'rank'), 'cuts')  407 us
    reduce_scatter x1, waiting for transfers between devices, on_device(): lax.psum_scatter(jnp.einsum('ba,ank->bnk', local_carry, core_two, precisi...  84.9 us
    psum x1, blocking collectives, on_device(): bridge_rows = lax.psum(part_bridge, 'cuts')  50.9 us
    another operation x6, other arithmetic, orthonormalize(): factor = jnp.linalg.cholesky(gram)  24.8 us
    all_gather x1, blocking collectives, on_device(): lax.all_gather(bridge_rows, 'rank', axis=0, tiled=True)  23.8 us
  transfers between devices with their start and end apart: 7, of which 7 were waited for; matrix products, arithmetic and copies ran while one was open for 0% of the time, Pallas kernels for 0%

profile of v1, /device:TPU:2, one launch (start us, length us, event | category | flops | bytes accessed | tf_op | source)
XLA Modules:
  0.0 1140.6 jit_solution(18053771619772361479)
XLA Ops:
  7.2 0.0 copy-start
  7.2 0.0 copy-start.1
  7.2 0.0 all-reduce.7.cloned.1.call-start
  7.2 1.3 copy-done
  8.5 2.1 fusion
  10.6 0.0 copy-done.1
  10.6 1.4 convolution_bitcast_fusion
  12.0 50.9 %psum.49 = f32[32,128]{1,0:T(8,128)S(1)} all-reduce(f32[32,128]{1,0:T(8,128)S(1)} %convolution_bitcast_fusion), channel_id=1, replica_groups=mesh['cuts'=16,'rank'=16] {'cuts'}, use_global_device_ids=true, to_apply=%region_0.0 | all-reduce | flops 4096 | bytes 32768 | tf_op jit(solution)/shard_map/psum | solution.py:32
  62.9 23.8 %all_gather.3 = f32[512,128]{1,0:T(8,128)S(1)} all-gather(f32[32,128]{1,0:T(8,128)S(1)} %psum.49), channel_id=1, replica_groups=mesh['cuts'=16,'rank'=16] {'rank'}, dimensions={0}, use_global_device_ids=true | all-gather | bytes 278528 | tf_op jit(solution)/shard_map/all_gather | solution.py:36
  86.7 3.2 copy.13
  89.9 1.5 reshape.29
  91.4 1.6 fusion.14
  92.9 1.1 fusion.15
  94.0 0.0 all-reduce.7.cloned.1.call-update
  94.1 0.2 all-reduce.9.cloned.1.call-start
  94.3 236.5 %all-reduce.7.cloned.1.call-done = f32[128,128]{0,1:T(8,128)} async-done(((f32[128,128]{0,1:T(8,128)}), f32[128,128]{0,1:T(8,128)}) %all-reduce.7.cloned.1.call-update) | async-done | bytes 65552 | tf_op jit(solution)/shard_map/psum | solution.py:16
  330.8 0.9 copy.15
  331.8 0.9 fusion.9
  332.6 11.7 %cholesky.44 = f32[128,128]{1,0:T(8,128)S(1)} custom-call(f32[128,128]{1,0:T(8,128)S(1)} %fusion.9), custom_call_target="Cholesky" | custom-call | tf_op jit(solution)/shard_map/jit(cholesky)/cholesky | solution.py:17
  344.4 0.6 compare_reduce_fusion.1
  345.0 0.7 fusion.2
  345.7 9.8 custom-call.8
  355.5 0.7 broadcast_multiply_fusion
  356.2 3.0 fusion.16
  359.2 0.0 all-reduce.9.cloned.1.call-update
  359.2 0.0 all-reduce.11.cloned.1.call-start
  359.2 92.1 %all-reduce.9.cloned.1.call-done = f32[128,512]{0,1:T(8,128)} async-done(((f32[128,512]{0,1:T(8,128)}), f32[128,512]{0,1:T(8,128)}) %all-reduce.9.cloned.1.call-update) | async-done | bytes 262160 | tf_op jit(solution)/shard_map/psum | solution.py:21
  451.4 0.0 all-reduce.11.cloned.1.call-update
  451.4 0.0 reduce-scatter.2.cloned.1.call-start
  451.4 112.0 %all-reduce.11.cloned.1.call-done = f32[128,512]{0,1:T(8,128)} async-done(((f32[128,512]{0,1:T(8,128)}), f32[128,512]{0,1:T(8,128)}) %all-reduce.11.cloned.1.call-update) | async-done | bytes 262160 | tf_op jit(solution)/shard_map/psum | solution.py:21
  563.5 6.8 fusion.10
  570.2 0.0 reduce-scatter.2.cloned.1.call-update
  570.3 0.0 copy-start.2
  570.3 0.3 all-reduce.13.cloned.1.call-start
  570.6 84.9 %reduce-scatter.2.cloned.1.call-done = f32[8,20,512]{2,0,1:T(8,128)} async-done(((f32[128,20,512]{2,0,1:T(8,128)}), f32[8,20,512]{2,0,1:T(8,128)}) %reduce-scatter.2.cloned.1.call-update) | async-done | bytes 327696 | tf_op jit(solution)/shard_map/reduce_scatter | solution.py:48
  655.4 1.2 copy.16
  656.7 0.0 copy-done.2
  656.7 0.4 fusion.17
  657.1 1.1 fusion.18
  658.2 0.0 all-reduce.13.cloned.1.call-update
  658.2 0.0 all-reduce.15.cloned.1.call-start
  658.2 243.5 %all-reduce.13.cloned.1.call-done = f32[128,128]{0,1:T(8,128)} async-done(((f32[128,128]{0,1:T(8,128)}), f32[128,128]{0,1:T(8,128)}) %all-reduce.13.cloned.1.call-update) | async-done | bytes 65552 | tf_op jit(solution)/shard_map/psum | solution.py:16
  901.8 0.9 copy.18
  902.7 0.9 fusion.6
  903.6 11.7 %cholesky.55 = f32[128,128]{1,0:T(8,128)S(1)} custom-call(f32[128,128]{1,0:T(8,128)S(1)} %fusion.6), custom_call_target="Cholesky" | custom-call | tf_op jit(solution)/shard_map/jit(cholesky)/cholesky | solution.py:17
  915.3 0.6 compare_reduce_fusion
  915.9 0.7 fusion.3
  916.6 9.8 custom-call.9
  926.4 0.2 broadcast_multiply_fusion.1
  926.7 1.1 fusion.19
  927.8 0.0 all-reduce.15.cloned.1.call-update
  927.8 0.0 all-reduce.17.cloned.1.call-start
  927.9 92.1 %all-reduce.15.cloned.1.call-done = f32[128,512]{1,0:T(8,128)} async-done(((f32[128,512]{1,0:T(8,128)}), f32[128,512]{1,0:T(8,128)}) %all-reduce.15.cloned.1.call-update) | async-done | bytes 262160 | tf_op jit(solution)/shard_map/psum | solution.py:21
  1020.0 0.0 all-reduce.17.cloned.1.call-update
  1020.1 0.8 copy.19
  1020.9 0.7 copy.20
  1021.5 110.6 %all-reduce.17.cloned.1.call-done = f32[128,512]{1,0:T(8,128)} async-done(((f32[128,512]{1,0:T(8,128)}), f32[128,512]{1,0:T(8,128)}) %all-reduce.17.cloned.1.call-update) | async-done | bytes 262160 | tf_op jit(solution)/shard_map/psum | solution.py:21
  1132.1 1.7 copy.31
  (5 shorter events, 0.1 us)
Async XLA Ops:
  7.2 1.3 copy-start
  7.2 3.4 copy-start.1
  7.2 323.6 %all-reduce.7.cloned.1.call-start = ((), (), s32[]{:S(2)}) async-start(), calls=%async_computation.1 | async-start | bytes 131072 | tf_op jit(solution)/shard_map/psum | solution.py:16
  94.1 357.3 %all-reduce.9.cloned.1.call-start = ((), (), s32[]{:S(2)}) async-start(), calls=%async_computation.2 | async-start | bytes 524288 | tf_op jit(solution)/shard_map/psum | solution.py:21
  359.2 204.3 %all-reduce.11.cloned.1.call-start = ((), (), s32[]{:S(2)}) async-start(), calls=%async_computation.3 | async-start | bytes 524288 | tf_op jit(solution)/shard_map/psum | solution.py:21
  451.4 204.1 %reduce-scatter.2.cloned.1.call-start = ((), (), s32[]{:S(2)}) async-start(), calls=%async_computation.4 | async-start | bytes 5570560 | tf_op jit(solution)/shard_map/reduce_scatter | solution.py:48
  570.3 86.4 %copy-start.2 = (f32[512,128]{1,0:T(8,128)S(1)}, f32[512,128]{1,0:T(8,128)}, u32[]{:S(2)}) copy-start(f32[512,128]{1,0:T(8,128)} %param.7) | copy-start | bytes 786436
  570.3 331.5 %all-reduce.13.cloned.1.call-start = ((), (), s32[]{:S(2)}) async-start(), calls=%async_computation.5 | async-start | bytes 131072 | tf_op jit(solution)/shard_map/psum | solution.py:16
  658.2 361.8 %all-reduce.15.cloned.1.call-start = ((), (), s32[]{:S(2)}) async-start(), calls=%async_computation.6 | async-start | bytes 524288 | tf_op jit(solution)/shard_map/psum | solution.py:21
  927.8 204.3 %all-reduce.17.cloned.1.call-start = ((), (), s32[]{:S(2)}) async-start(), calls=%async_computation.7 | async-start | bytes 524288 | tf_op jit(solution)/shard_map/psum | solution.py:21
Sparse Core Ops, SparseCore 0:
  94.2 236.5 all-reduce.6
  359.3 92.0 all-reduce.8
  453.7 109.7 all-reduce.10
  570.4 85.0 reduce-scatter.1
  661.4 240.3 all-reduce.12
  927.9 92.0 all-reduce.14
  1022.3 109.7 all-reduce.16

commit v2 on v0

--- a/solution.py
+++ b/solution.py
@@ -13,7 +13,7 @@
     local_gram = jnp.dot(
         own_rows.T, own_rows, precision=highest, preferred_element_type=jnp.float32
     )
-    gram = lax.psum(local_gram, ("cuts", "rank"))
+    gram = lax.psum(lax.psum(local_gram, "cuts"), "rank")
     factor = jnp.linalg.cholesky(gram)
     ortho = lax.linalg.triangular_solve(
         factor, all_rows, left_side=False, lower=True, transpose_a=True

time: 1230 us -> 1140 us (0.927)
  waiting for transfers between devices: 1070 us -> 974 us
    psum x2 -> x4, waiting for transfers between devices: 480 us -> 384 us  [orthonormalize(): gram = lax.psum(lax.psum(local_gram, 'cuts'), 'rank')]
  transfers between devices with their start and end apart: 5 -> 7, of which waited for: 5 -> 7; matrix products, arithmetic and copies ran while one was open for 0% -> 0% of each run, Pallas kernels for 0% -> 0%
where the time goes in v2:
time: 1140 us
  waiting for transfers between devices  974 us (85%)
  blocking collectives  74.6 us (7%)
  other arithmetic  47.4 us (4%)
  matrix products  19.5 us (2%)
  between operations  14.3 us (1%)
  local copies, waits for them, and re-layouts  12.2 us (1%)
    psum x2, waiting for transfers between devices, orthonormalize(): carried = lax.psum(carry_of(ortho), ('cuts', 'rank'))  507 us
    psum x4, waiting for transfers between devices, orthonormalize(): gram = lax.psum(lax.psum(local_gram, 'cuts'), 'rank')  384 us
    reduce_scatter x1, waiting for transfers between devices, on_device(): lax.psum_scatter(jnp.einsum('ba,ank->bnk', local_carry, core_two, precisi...  83.2 us
    psum x1, blocking collectives, on_device(): bridge_rows = lax.psum(part_bridge, 'cuts')  50.9 us
    another operation x6, other arithmetic, orthonormalize(): factor = jnp.linalg.cholesky(gram)  24.8 us
    all_gather x1, blocking collectives, on_device(): lax.all_gather(bridge_rows, 'rank', axis=0, tiled=True)  23.8 us
  transfers between devices with their start and end apart: 7, of which 7 were waited for; matrix products, arithmetic and copies ran while one was open for 0% of the time, Pallas kernels for 0%

profile of v2, /device:TPU:2, one launch (start us, length us, event | category | flops | bytes accessed | tf_op | source)
XLA Modules:
  0.0 1142.7 jit_solution(18340750666477256698)
XLA Ops:
  7.2 0.0 copy-start
  7.2 0.0 copy-start.1
  7.2 0.0 all-reduce.7.cloned.1.call-start
  7.2 1.3 copy-done
  8.5 2.1 fusion
  10.6 0.0 copy-done.1
  10.6 1.4 convolution_bitcast_fusion
  12.0 50.9 %psum.49 = f32[32,128]{1,0:T(8,128)S(1)} all-reduce(f32[32,128]{1,0:T(8,128)S(1)} %convolution_bitcast_fusion), channel_id=1, replica_groups=mesh['cuts'=16,'rank'=16] {'cuts'}, use_global_device_ids=true, to_apply=%region_0.0 | all-reduce | flops 4096 | bytes 32768 | tf_op jit(solution)/shard_map/psum | solution.py:32
  62.9 23.8 %all_gather.3 = f32[512,128]{1,0:T(8,128)S(1)} all-gather(f32[32,128]{1,0:T(8,128)S(1)} %psum.49), channel_id=1, replica_groups=mesh['cuts'=16,'rank'=16] {'rank'}, dimensions={0}, use_global_device_ids=true | all-gather | bytes 278528 | tf_op jit(solution)/shard_map/all_gather | solution.py:36
  86.7 3.2 copy.13
  89.9 1.5 reshape.29
  91.4 1.6 fusion.14
  92.9 1.1 fusion.15
  94.0 0.0 all-reduce.7.cloned.1.call-update
  94.1 0.0 all-reduce.9.cloned.1.call-start
  94.1 96.5 %all-reduce.7.cloned.1.call-done = f32[128,128]{0,1:T(8,128)} async-done(((f32[128,128]{0,1:T(8,128)}), f32[128,128]{0,1:T(8,128)}) %all-reduce.7.cloned.1.call-update) | async-done | bytes 65552 | tf_op jit(solution)/shard_map/psum | solution.py:16
  190.6 0.0 all-reduce.9.cloned.1.call-update
  190.7 0.2 all-reduce.11.cloned.1.call-start
  190.9 93.5 %all-reduce.9.cloned.1.call-done = f32[128,128]{0,1:T(8,128)} async-done(((f32[128,128]{0,1:T(8,128)}), f32[128,128]{0,1:T(8,128)}) %all-reduce.9.cloned.1.call-update) | async-done | bytes 65552 | tf_op jit(solution)/shard_map/psum | solution.py:16
  284.4 0.9 copy.15
  285.4 0.9 fusion.9
  286.2 11.7 %cholesky.44 = f32[128,128]{1,0:T(8,128)S(1)} custom-call(f32[128,128]{1,0:T(8,128)S(1)} %fusion.9), custom_call_target="Cholesky" | custom-call | tf_op jit(solution)/shard_map/jit(cholesky)/cholesky | solution.py:17
  298.0 0.6 compare_reduce_fusion.1
  298.6 0.7 fusion.2
  299.3 9.8 custom-call.8
  309.1 0.7 broadcast_multiply_fusion
  309.8 3.0 fusion.16
  312.8 0.0 all-reduce.11.cloned.1.call-update
  312.8 0.0 reduce-scatter.2.cloned.1.call-start
  312.8 254.1 %all-reduce.11.cloned.1.call-done = f32[128,512]{0,1:T(8,128)} async-done(((f32[128,512]{0,1:T(8,128)}), f32[128,512]{0,1:T(8,128)}) %all-reduce.11.cloned.1.call-update) | async-done | bytes 262160 | tf_op jit(solution)/shard_map/psum | solution.py:21
  567.0 6.8 fusion.10
  573.8 0.0 reduce-scatter.2.cloned.1.call-update
  573.8 0.0 copy-start.2
  573.8 0.3 all-reduce.13.cloned.1.call-start
  574.1 83.2 %reduce-scatter.2.cloned.1.call-done = f32[8,20,512]{2,0,1:T(8,128)} async-done(((f32[128,20,512]{2,0,1:T(8,128)}), f32[8,20,512]{2,0,1:T(8,128)}) %reduce-scatter.2.cloned.1.call-update) | async-done | bytes 327696 | tf_op jit(solution)/shard_map/reduce_scatter | solution.py:48
  657.3 1.2 copy.16
  658.5 0.0 copy-done.2
  658.5 0.4 fusion.17
  658.9 1.1 fusion.18
  660.0 0.0 all-reduce.13.cloned.1.call-update
  660.0 0.0 all-reduce.15.cloned.1.call-start
  660.0 100.2 %all-reduce.13.cloned.1.call-done = f32[128,128]{0,1:T(8,128)} async-done(((f32[128,128]{0,1:T(8,128)}), f32[128,128]{0,1:T(8,128)}) %all-reduce.13.cloned.1.call-update) | async-done | bytes 65552 | tf_op jit(solution)/shard_map/psum | solution.py:16
  760.3 0.0 all-reduce.15.cloned.1.call-update
  760.3 0.0 all-reduce.17.cloned.1.call-start
  760.3 93.6 %all-reduce.15.cloned.1.call-done = f32[128,128]{0,1:T(8,128)} async-done(((f32[128,128]{0,1:T(8,128)}), f32[128,128]{0,1:T(8,128)}) %all-reduce.15.cloned.1.call-update) | async-done | bytes 65552 | tf_op jit(solution)/shard_map/psum | solution.py:16
  853.9 0.9 copy.18
  854.8 0.9 fusion.6
  855.7 11.7 %cholesky.55 = f32[128,128]{1,0:T(8,128)S(1)} custom-call(f32[128,128]{1,0:T(8,128)S(1)} %fusion.6), custom_call_target="Cholesky" | custom-call | tf_op jit(solution)/shard_map/jit(cholesky)/cholesky | solution.py:17
  867.5 0.6 compare_reduce_fusion
  868.1 0.7 fusion.3
  868.8 9.8 custom-call.9
  878.6 0.2 broadcast_multiply_fusion.1
  878.8 1.1 fusion.19
  879.9 0.0 all-reduce.17.cloned.1.call-update
  880.0 0.8 copy.19
  880.8 0.7 copy.20
  881.5 252.7 %all-reduce.17.cloned.1.call-done = f32[128,512]{1,0:T(8,128)} async-done(((f32[128,512]{1,0:T(8,128)}), f32[128,512]{1,0:T(8,128)}) %all-reduce.17.cloned.1.call-update) | async-done | bytes 262160 | tf_op jit(solution)/shard_map/psum | solution.py:21
  1134.1 1.7 copy.31
  (5 shorter events, 0.1 us)
Async XLA Ops:
  7.2 1.3 copy-start
  7.2 3.4 copy-start.1
  7.2 183.5 %all-reduce.7.cloned.1.call-start = ((), (), s32[]{:S(2)}) async-start(), calls=%async_computation.1 | async-start | bytes 131072 | tf_op jit(solution)/shard_map/psum | solution.py:16
  94.1 190.4 %all-reduce.9.cloned.1.call-start = ((), (), s32[]{:S(2)}) async-start(), calls=%async_computation.2 | async-start | bytes 131072 | tf_op jit(solution)/shard_map/psum | solution.py:16
  190.7 376.3 %all-reduce.11.cloned.1.call-start = ((), (), s32[]{:S(2)}) async-start(), calls=%async_computation.3 | async-start | bytes 524288 | tf_op jit(solution)/shard_map/psum | solution.py:21
  312.8 344.5 %reduce-scatter.2.cloned.1.call-start = ((), (), s32[]{:S(2)}) async-start(), calls=%async_computation.4 | async-start | bytes 5570560 | tf_op jit(solution)/shard_map/reduce_scatter | solution.py:48
  573.8 84.7 %copy-start.2 = (f32[512,128]{1,0:T(8,128)S(1)}, f32[512,128]{1,0:T(8,128)}, u32[]{:S(2)}) copy-start(f32[512,128]{1,0:T(8,128)} %param.7) | copy-start | bytes 786436
  573.8 186.5 %all-reduce.13.cloned.1.call-start = ((), (), s32[]{:S(2)}) async-start(), calls=%async_computation.5 | async-start | bytes 131072 | tf_op jit(solution)/shard_map/psum | solution.py:16
  660.0 193.9 %all-reduce.15.cloned.1.call-start = ((), (), s32[]{:S(2)}) async-start(), calls=%async_computation.6 | async-start | bytes 131072 | tf_op jit(solution)/shard_map/psum | solution.py:16
  760.3 373.8 %all-reduce.17.cloned.1.call-start = ((), (), s32[]{:S(2)}) async-start(), calls=%async_computation.7 | async-start | bytes 524288 | tf_op jit(solution)/shard_map/psum | solution.py:21
Sparse Core Ops, SparseCore 0:
  94.2 96.4 all-reduce.6
  193.8 90.5 all-reduce.8
  312.9 254.0 all-reduce.10
  573.9 83.3 reduce-scatter.1
  660.1 100.1 all-reduce.12
  763.3 90.5 all-reduce.14
  880.1 254.0 all-reduce.16
